TPU v7x, 32 devices: a whole 2x2x4 slice. The times are simulated.
32 devices in a mesh: row: 4 (over z), col: 2 (over x), depth: 4 (over y, core).
Axes of the slice: x: 2, y: 2, z: 4, core: 2. Of those that a mesh axis runs over, the one named last changes fastest.
Arguments:
- tokens: bfloat16 [2560, 8192], P(('row', 'depth'), 'col'), may hold values from -6 to 6
- weight: bfloat16 [8192, 4096], P('row', 'col'), may hold values from -0.0625 to 0.0625
- cotangent: bfloat16 [2560, 4096], P(('row', 'depth'), 'col'), may hold values from -6 to 6
- master: float32 [8192, 4096], P(('row', 'depth'), 'col'), may hold values from -0.1 to 0.1
- first_moment: float32 [8192, 4096], P(('row', 'depth'), 'col'), may hold values from -6 to 6
- second_moment: float32 [8192, 4096], P(('row', 'depth'), 'col'), may hold values from 0.1 to 10
Outputs:
- queries: bfloat16 [2560, 4096], P(('row', 'depth'), 'col')
- token_grad: bfloat16 [2560, 8192], P(('row', 'depth'), 'col')
- new_master: float32 [8192, 4096], P(('row', 'depth'), 'col')
- new_first: float32 [8192, 4096], P(('row', 'depth'), 'col')
- new_second: float32 [8192, 4096], P(('row', 'depth'), 'col')
- new_weight: bfloat16 [8192, 4096], P('row', 'col')
All inputs are finite; a program needn't handle non-finite values.
Results may differ from a plain program's by a relative error of at most 0.001.
Values may be sent and summed in bfloat16 or wider, within the bound.
A program may use at most 128 MiB of HBM per device.

v0:
```python
import math
import jax
import jax.numpy as jnp
from jax import lax
from jax.sharding import PartitionSpec as P

beta_one = 0.9
beta_two = 0.95
learn_rate = 0.02
decay_rate = 0.1
adam_eps = 1e-08
bias_one = 1.0 - 0.9**50
bias_two = 1.0 - 0.95**50


def local(tokens, weight, cotangent, master, first_moment, second_moment):
    rows, cols = (lax.axis_size("row"), lax.axis_size("col"))
    block = tokens.shape[0]
    total_tokens = block * rows * lax.axis_size("depth")
    grad_scale = 1.0 / math.sqrt(total_tokens)
    full_rows = lax.all_gather(tokens, "col", axis=1, tiled=True)
    line_cotangent = lax.all_gather(cotangent, "row", axis=0, tiled=True)
    line_tokens = lax.all_to_all(full_rows, "row", split_axis=1, concat_axis=0, tiled=True)
    partial_grad = lax.dot_general(
        line_cotangent, weight, (((1,), (1,)), ((), ())), preferred_element_type=jnp.float32
    )
    piece = lax.psum_scatter(partial_grad, "col", scatter_dimension=1, tiled=True).astype(
        jnp.bfloat16
    )
    partial_queries = jnp.dot(line_tokens, weight, preferred_element_type=jnp.float32)
    queries = lax.psum_scatter(partial_queries, "row", scatter_dimension=0, tiled=True).astype(
        jnp.bfloat16
    )
    piece = lax.all_to_all(
        piece.reshape(rows, block, -1), "row", split_axis=0, concat_axis=0, tiled=True
    )
    piece = lax.all_to_all(
        piece.reshape(cols, rows // cols, block, -1), "col", split_axis=0, concat_axis=0, tiled=True
    )
    token_grad = piece.transpose(2, 1, 0, 3).reshape(tokens.shape)
    token_slab = lax.all_to_all(line_tokens, "depth", split_axis=1, concat_axis=0, tiled=True)
    all_cotangent = lax.all_gather(line_cotangent, "depth", axis=0, tiled=True)
    product = lax.dot_general(
        token_slab, all_cotangent, (((0,), (0,)), ((), ())), preferred_element_type=jnp.float32
    )
    grad = product * grad_scale
    new_first = beta_one * first_moment + (1.0 - beta_one) * grad
    new_second = beta_two * second_moment + (1.0 - beta_two) * grad * grad
    step_value = new_first / bias_one / (jnp.sqrt(new_second / bias_two) + adam_eps)
    new_master = master - learn_rate * (step_value + decay_rate * master)
    shard_weight = new_master.astype(jnp.bfloat16)
    new_weight = lax.all_gather(shard_weight, "depth", axis=0, tiled=True)
    return (queries, token_grad, new_master, new_first, new_second, new_weight)


def solution(mesh):
    in_specs = (
        P(("row", "depth"), "col"),
        P("row", "col"),
        P(("row", "depth"), "col"),
        P(("row", "depth"), "col"),
        P(("row", "depth"), "col"),
        P(("row", "depth"), "col"),
    )
    out_specs = (
        P(("row", "depth"), "col"),
        P(("row", "depth"), "col"),
        P(("row", "depth"), "col"),
        P(("row", "depth"), "col"),
        P(("row", "depth"), "col"),
        P("row", "col"),
    )
    return jax.shard_map(local, mesh=mesh, in_specs=in_specs, out_specs=out_specs, check_vma=False)
```

profile of v0, /device:TPU:0, one launch (start us, length us, event | category | flops | bytes accessed | tf_op | source)
XLA Modules:
  0.0 441.7 jit_solution(11255023881615150435)
XLA Ops:
  7.2 0.0 all-gather.7.cloned.1.call-start
  7.2 0.7 all-gather.7.cloned.1.call-update
  7.9 0.0 all-gather.5.cloned.1.call-start
  7.9 0.7 all-gather.5.cloned.1.call-update
  8.6 0.0 all-gather.9.cloned.1.call-start
  8.7 58.3 %all-gather.7.cloned.1.call-done = bf16[640,2048]{1,0:T(8,128)(2,1)} async-done(((bf16[160,2048]{1,0:T(8,128)(2,1)}), bf16[640,2048]{1,0:T(8,128)(2,1)}) %all-gather.7.cloned.1.call-update) | async-done | bytes 2621456 | tf_op jit(solution)/shard_map/all_gather | solution.py:22
  67.0 0.0 all-gather.9.cloned.1.call-update
  67.1 0.0 reduce-scatter.5.cloned.1.call-start
  67.1 11.1 %fusion.2 = f32[640,2048]{1,0:T(8,128)} fusion(bf16[640,2048]{1,0:T(8,128)(2,1)} %all-gather.7.cloned.1.call-done, bf16[2048,2048]{1,0:T(8,128)(2,1)} %param.7), kind=kOutput, calls=%fused_computation.6 | convolution fusion | flops 5368709120 | bytes 16252928 | tf_op jit(solution)/shard_map/dot_general | solution.py:24
  78.2 0.0 reduce-scatter.5.cloned.1.call-update
  78.2 0.0 reduce-scatter.3.cloned.1.call-start
  78.3 28.1 %all-gather.5.cloned.1.call-done = bf16[160,8192]{1,0:T(8,128)(2,1)} async-done(((bf16[160,4096]{1,0:T(8,128)(2,1)}), bf16[160,8192]{1,0:T(8,128)(2,1)}) %all-gather.5.cloned.1.call-update) | async-done | bytes 2621456 | tf_op jit(solution)/shard_map/all_gather | solution.py:21
  106.4 2.1 copy.27
  108.4 63.7 %all_to_all.48 = bf16[160,4,2048]{2,0,1:T(8,128)(2,1)S(1)} all-to-all(bf16[160,4,2048]{2,0,1:T(8,128)(2,1)S(1)} %bitcast.21), channel_id=1, replica_groups=mesh['row'=4,'col'=2,'depth'=4] {'row'}, dimensions={1} | all-to-all | bytes 5242880 | tf_op jit(solution)/shard_map/all_to_all | solution.py:23
  172.1 9.4 %fusion.1 = f32[640,2048]{1,0:T(8,128)} fusion(bf16[640,2048]{1,0:T(8,128)(2,1)S(1)} %bitcast.19, bf16[2048,2048]{1,0:T(8,128)(2,1)} %param.7), kind=kOutput, calls=%fused_computation.5 | convolution fusion | flops 5368709120 | bytes 16252928 | tf_op jit(solution)/shard_map/dot_general | solution.py:30
  181.5 0.0 reduce-scatter.3.cloned.1.call-update
  181.6 0.0 all-gather.11.cloned.1.call-start
  181.6 3.5 all_to_all.40
  185.2 2.9 copy.24
  188.1 33.8 %all_to_all.49 = bf16[640,4,512]{2,0,1:T(8,128)(2,1)S(1)} all-to-all(bf16[640,4,512]{2,0,1:T(8,128)(2,1)S(1)} %copy.24), channel_id=1, replica_groups=mesh['row'=4,'col'=2,'depth'=4] {'depth'}, dimensions={1} | all-to-all | bytes 5242880 | tf_op jit(solution)/shard_map/all_to_all | solution.py:41
  221.8 0.0 all-gather.9.cloned.1.call-done
  221.9 18.4 %fusion = (bf16[512,2048]{1,0:T(8,128)(2,1)}, f32[512,2048]{1,0:T(8,128)}, f32[512,2048]{1,0:T(8,128)}, f32[512,2048]{1,0:T(8,128)}) fusion(f32[512,2048]{1,0:T(8,128)} %param.9, f32[512,2048]{1,0:T(8,128)} %param.10, f32[512,2048]{1,0:T(8,128)} %param.11, bf16[2560,512]{1,0:T(8,128)(2,1)S(1)} %bitcast.26, bf16[2560,2048]{1,0:T(8,128)(2,1)} %all-gather.9.cloned.1.call-done), kind=kOutput, calls=%fused_computation.4 | convolution fusion | flops 5386534912 | bytes 40370176 | tf_op jit(solution)/shard_map/dot_general | solution.py:43
  240.3 0.0 all-gather.11.cloned.1.call-update
  240.3 5.8 %reduce-scatter.5.cloned.1.call-done = f32[640,1024]{1,0:T(8,128)} async-done(((f32[640,2048]{1,0:T(8,128)}), f32[640,1024]{1,0:T(8,128)}) %reduce-scatter.5.cloned.1.call-update) | async-done | bytes 2621456 | tf_op jit(solution)/shard_map/reduce_scatter | solution.py:27
  246.1 1.9 convert_element_type.10
  248.0 70.7 %all_to_all.50 = bf16[4,160,1024]{2,1,0:T(8,128)(2,1)S(1)} all-to-all(bf16[4,160,1024]{2,1,0:T(8,128)(2,1)S(1)} %bitcast.24), channel_id=1, replica_groups=mesh['row'=4,'col'=2,'depth'=4] {'row'}, dimensions={0} | all-to-all | bytes 2621440 | tf_op jit(solution)/shard_map/all_to_all | solution.py:34
  318.7 1.3 copy.22
  320.1 13.3 %all_to_all.51 = bf16[2,2,160,1024]{3,1,2,0:T(2,128)(2,1)S(1)} all-to-all(bf16[2,2,160,1024]{3,1,2,0:T(2,128)(2,1)S(1)} %copy.22), channel_id=1, replica_groups=mesh['row'=4,'col'=2,'depth'=4] {'col'}, dimensions={0} | all-to-all | bytes 2621440 | tf_op jit(solution)/shard_map/all_to_all | solution.py:37
  333.3 2.0 copy.23
  335.4 1.8 reshape.30
  337.2 24.3 %reduce-scatter.3.cloned.1.call-done = f32[160,2048]{1,0:T(8,128)} async-done(((f32[640,2048]{1,0:T(8,128)}), f32[160,2048]{1,0:T(8,128)}) %reduce-scatter.3.cloned.1.call-update) | async-done | bytes 1310736 | tf_op jit(solution)/shard_map/reduce_scatter | solution.py:31
  361.5 2.2 convert_element_type.9
  363.8 62.7 %all-gather.11.cloned.1.call-done = bf16[2048,2048]{1,0:T(8,128)(2,1)} async-done(((bf16[512,2048]{1,0:T(8,128)(2,1)}), bf16[2048,2048]{1,0:T(8,128)(2,1)}) %all-gather.11.cloned.1.call-update) | async-done | bytes 8388624 | tf_op jit(solution)/shard_map/all_gather | solution.py:52
  426.4 8.4 %copy.29 = bf16[2048,2048]{1,0:T(8,128)(2,1)} copy(bf16[2048,2048]{1,0:T(8,128)(2,1)} %all-gather.11.cloned.1.call-done) | data formatting | bytes 16777216
Async XLA Ops:
  7.2 59.9 %all-gather.7.cloned.1.call-start = ((), (), s32[]{:S(2)}) async-start(), calls=%async_computation.8 | async-start | bytes 3276800 | tf_op jit(solution)/shard_map/all_gather | solution.py:22
  7.9 98.5 %all-gather.5.cloned.1.call-start = ((), (), s32[]{:S(2)}) async-start(), calls=%async_computation.6 | async-start | bytes 3932160 | tf_op jit(solution)/shard_map/all_gather | solution.py:21
  8.6 213.2 %all-gather.9.cloned.1.call-start = ((), (), s32[]{:S(2)}) async-start(), calls=%async_computation.10 | async-start | bytes 13107200 | tf_op jit(solution)/shard_map/all_gather | solution.py:42
  67.1 179.0 %reduce-scatter.5.cloned.1.call-start = ((), (), s32[]{:S(2)}) async-start(), calls=%async_computation.9 | async-start | bytes 7864320 | tf_op jit(solution)/shard_map/reduce_scatter | solution.py:27
  78.2 283.3 %reduce-scatter.3.cloned.1.call-start = ((), (), s32[]{:S(2)}) async-start(), calls=%async_computation.7 | async-start | bytes 6553600 | tf_op jit(solution)/shard_map/reduce_scatter | solution.py:31
  181.6 244.9 %all-gather.11.cloned.1.call-start = ((), (), s32[]{:S(2)}) async-start(), calls=%async_computation.11 | async-start | bytes 10485760 | tf_op jit(solution)/shard_map/all_gather | solution.py:52
Sparse Core Ops, SparseCore 0:
  9.5 57.4 all-gather.6
  68.6 37.7 all-gather.4
  107.9 70.1 all-gather.8
  180.3 65.7 reduce-scatter.4
  248.8 112.6 reduce-scatter.2
  362.9 63.4 all-gather.10
where the time goes:
time: 442 us
  waiting for transfers between devices  181 us (41%)
  blocking collectives  181 us (41%)
  matrix products  39 us (9%)
  local copies, waits for them, and re-layouts  22.1 us (5%)
  between operations  14.1 us (3%)
    all_to_all x1, blocking collectives, local(): lax.all_to_all(piece.reshape(rows, block, -1), 'row', split_axis=0, conca...  70.7 us
    all_to_all x1, blocking collectives, local(): lax.all_to_all(full_rows, 'row', split_axis=1, concat_axis=0, tiled=True)  63.7 us
    all_gather x1, waiting for transfers between devices, local(): new_weight = lax.all_gather(shard_weight, 'depth', axis=0, tiled=True)  62.7 us
    all_gather x1, waiting for transfers between devices, local(): line_cotangent = lax.all_gather(cotangent, 'row', axis=0, tiled=True)  58.3 us
    all_to_all x1, blocking collectives, local(): lax.all_to_all(line_tokens, 'depth', split_axis=1, concat_axis=0, tiled=T...  33.8 us
    all_gather x1, waiting for transfers between devices, local(): full_rows = lax.all_gather(tokens, 'col', axis=1, tiled=True)  28.1 us
    reduce_scatter x1, waiting for transfers between devices, local(): lax.psum_scatter(partial_queries, 'row', scatter_dimension=0, tiled=True)  24.3 us
    dot_general x1, matrix products, local(): lax.dot_general(token_slab, all_cotangent, (((0,), (0,)), ((), ())), pref...  18.4 us
  transfers between devices with their start and end apart: 6, of which 5 were waited for; matrix products, arithmetic and copies ran while one was open for 12% of the time, Pallas kernels for 0%

commit v1 on v0

--- a/solution.py
+++ b/solution.py
@@ -19,7 +19,12 @@
     total_tokens = block * rows * lax.axis_size("depth")
     grad_scale = 1.0 / math.sqrt(total_tokens)
     full_rows = lax.all_gather(tokens, "col", axis=1, tiled=True)
-    line_cotangent = lax.all_gather(cotangent, "row", axis=0, tiled=True)
+    ring = [cotangent]
+    for hop in range(3):
+        ring.append(lax.ppermute(ring[-1], "row", [(dev, (dev + 1) % 4) for dev in range(4)]))
+    line_cotangent = jnp.roll(
+        jnp.concatenate(ring[::-1], axis=0), (lax.axis_index("row") + 1) * ring[0].shape[0], axis=0
+    )
     line_tokens = lax.all_to_all(full_rows, "row", split_axis=1, concat_axis=0, tiled=True)
     partial_grad = lax.dot_general(
         line_cotangent, weight, (((1,), (1,)), ((), ())), preferred_element_type=jnp.float32

time: 442 us -> 425 us (0.962)
  local copies, waits for them, and re-layouts: 22.1 us -> 62.4 us
  blocking collectives: 181 us -> 148 us
  waiting for transfers between devices: 181 us -> 150 us
  starting transfers between devices: 0.24 us -> 7.15 us
    all_gather x1 -> x0, waiting for transfers between devices: 58.3 us -> none  [local(): line_cotangent = lax.all_gather(cotangent, 'row', axis=0, tiled=True)]
    ppermute x0 -> x3, waiting for transfers between devices: none -> 51.4 us  [local(): lax.ppermute(ring[-1], 'row', [(dev, (dev + 1) % 4) for dev in range(4)])]
    unnamed x1 -> x16, local copies, waits for them, and re-layouts: 8.44 us -> 45.1 us
    all_to_all x1 -> x0, blocking collectives: 33.8 us -> none  [local(): lax.all_to_all(line_tokens, 'depth', split_axis=1, concat_axis=0, tiled=T...]
    all_gather x1, waiting for transfers between devices: 28.1 us -> 9.71 us  [local(): full_rows = lax.all_gather(tokens, 'col', axis=1, tiled=True)]
    all_gather x1, waiting for transfers between devices: 62.7 us -> 46.2 us  [local(): new_weight = lax.all_gather(shard_weight, 'depth', axis=0, tiled=True)]
    all_to_all x0 -> x1, waiting for transfers between devices: none -> 14.8 us  [local(): lax.all_to_all(line_tokens, 'depth', split_axis=1, concat_axis=0, tiled=T...]
  transfers between devices with their start and end apart: 6 -> 9, of which waited for: 5 -> 8; matrix products, arithmetic and copies ran while one was open for 12% -> 21% of each run, Pallas kernels for 0% -> 0%
where the time goes in v1:
time: 425 us; the launch traced here: 424 us
  waiting for transfers between devices  150 us (35%)
  blocking collectives  148 us (35%)
  local copies, waits for them, and re-layouts  62.4 us (15%)
  matrix products  39.5 us (9%)
  between operations  13.9 us (3%)
  starting transfers between devices  7.15 us (2%)
    all_to_all x1, blocking collectives, local(): lax.all_to_all(piece.reshape(rows, block, -1), 'row', split_axis=0, conca...  70.7 us
    all_to_all x1, blocking collectives, local(): lax.all_to_all(full_rows, 'row', split_axis=1, concat_axis=0, tiled=True)  63.7 us
    ppermute x3, waiting for transfers between devices, local(): lax.ppermute(ring[-1], 'row', [(dev, (dev + 1) % 4) for dev in range(4)])  51.4 us
    all_gather x1, waiting for transfers between devices, local(): new_weight = lax.all_gather(shard_weight, 'depth', axis=0, tiled=True)  46.2 us
    unnamed x16, local copies, waits for them, and re-layouts  45.1 us
    reduce_scatter x1, waiting for transfers between devices, local(): lax.psum_scatter(partial_queries, 'row', scatter_dimension=0, tiled=True)  24.3 us
    dot_general x1, matrix products, local(): lax.dot_general(token_slab, all_cotangent, (((0,), (0,)), ((), ())), pref...  18.9 us
    all_to_all x1, waiting for transfers between devices, local(): lax.all_to_all(line_tokens, 'depth', split_axis=1, concat_axis=0, tiled=T...  14.8 us
  transfers between devices with their start and end apart: 9, of which 8 were waited for; matrix products, arithmetic and copies ran while one was open for 21% of the time, Pallas kernels for 0%

profile of v1, /device:TPU:0, one launch (start us, length us, event | category | flops | bytes accessed | tf_op | source)
XLA Modules:
  0.0 424.3 jit_solution(10655208818585960207)
XLA Ops:
  7.2 0.0 copy-start
  7.2 0.0 all-gather.4.cloned.1.call-start
  7.2 3.1 collective-permute-start
  10.3 17.0 %collective-permute-done = bf16[160,2048]{1,0:T(8,128)(2,1)S(1)} collective-permute-done((bf16[160,2048]{1,0:T(8,128)(2,1)}, bf16[160,2048]{1,0:T(8,128)(2,1)S(1)}, u32[]{:S(2)}, u32[]{:S(2)}) %collective-permute-start) | collective-permute-done | bytes 655392 | tf_op jit(solution)/shard_map/ppermute | solution.py:24
  27.3 0.0 collective-permute-start.1
  27.3 17.7 %collective-permute-done.1 = bf16[160,2048]{1,0:T(8,128)(2,1)S(1)} collective-permute-done((bf16[160,2048]{1,0:T(8,128)(2,1)S(1)}, bf16[160,2048]{1,0:T(8,128)(2,1)S(1)}, u32[]{:S(2)}, u32[]{:S(2)}) %collective-permute-start.1) | collective-permute-done | bytes 655392 | tf_op jit(solution)/shard_map/ppermute | solution.py:24
  45.0 0.0 collective-permute-start.2
  45.0 0.0 all-gather.4.cloned.1.call-update
  45.0 0.0 all-gather.6.cloned.1.call-start
  45.1 16.7 %collective-permute-done.2 = bf16[160,2048]{1,0:T(8,128)(2,1)S(1)} collective-permute-done((bf16[160,2048]{1,0:T(8,128)(2,1)S(1)}, bf16[160,2048]{1,0:T(8,128)(2,1)S(1)}, u32[]{:S(2)}, u32[]{:S(2)}) %collective-permute-start.2) | collective-permute-done | bytes 655392 | tf_op jit(solution)/shard_map/ppermute | solution.py:24
  62.0 0.0 copy-done
  62.3 2.2 constant_dynamic-slice_fusion
  64.5 0.0 all-gather.6.cloned.1.call-update
  64.5 0.0 reduce-scatter.5.cloned.1.call-start
  64.5 11.1 %fusion.2 = f32[640,2048]{1,0:T(8,128)} fusion(bf16[640,2048]{1,0:T(8,128)(2,1)} %constant_dynamic-slice_fusion, bf16[2048,2048]{1,0:T(8,128)(2,1)} %param.7), kind=kOutput, calls=%fused_computation.15 | convolution fusion | flops 5368709120 | bytes 16252928 | tf_op jit(solution)/shard_map/dot_general | solution.py:29
  75.6 0.0 reduce-scatter.5.cloned.1.call-update
  75.7 0.0 reduce-scatter.3.cloned.1.call-start
  75.7 9.7 %all-gather.4.cloned.1.call-done = bf16[160,8192]{1,0:T(8,128)(2,1)} async-done(((bf16[160,4096]{1,0:T(8,128)(2,1)}), bf16[160,8192]{1,0:T(8,128)(2,1)}) %all-gather.4.cloned.1.call-update) | async-done | bytes 2621456 | tf_op jit(solution)/shard_map/all_gather | solution.py:21
  85.4 2.1 copy.67
  87.5 63.7 %all_to_all.48 = bf16[160,4,2048]{2,0,1:T(8,128)(2,1)S(1)} all-to-all(bf16[160,4,2048]{2,0,1:T(8,128)(2,1)S(1)} %bitcast.27), channel_id=1, replica_groups=mesh['row'=4,'col'=2,'depth'=4] {'row'}, dimensions={1} | all-to-all | bytes 5242880 | tf_op jit(solution)/shard_map/all_to_all | solution.py:28
  151.1 9.4 %fusion.1 = f32[640,2048]{1,0:T(8,128)} fusion(bf16[640,2048]{1,0:T(8,128)(2,1)S(1)} %bitcast.25, bf16[2048,2048]{1,0:T(8,128)(2,1)} %param.7), kind=kOutput, calls=%fused_computation.14 | convolution fusion | flops 5368709120 | bytes 16252928 | tf_op jit(solution)/shard_map/dot_general | solution.py:35
  160.6 0.0 reduce-scatter.3.cloned.1.call-update
  160.6 3.5 all_to_all.40
  164.1 4.2 copy.57
  168.3 3.7 all-to-all-start.3
  172.0 0.2 all-gather.8.cloned.1.call-start
  172.2 5.3 %copy.60 = f32[512,2048]{0,1:T(8,128)} copy(f32[512,2048]{1,0:T(8,128)} %param.9) | data formatting | bytes 8388608 | tf_op args[3]
  177.6 5.3 %copy.56 = f32[512,2048]{0,1:T(8,128)} copy(f32[512,2048]{1,0:T(8,128)} %param.10) | data formatting | bytes 8388608 | tf_op args[4]
  182.9 5.5 %copy.58 = f32[512,2048]{0,1:T(8,128)} copy(f32[512,2048]{1,0:T(8,128)} %param.11) | data formatting | bytes 8388608 | tf_op args[5]
  188.4 14.8 %all-to-all-done.3 = bf16[640,4,512]{2,0,1:T(8,128)(2,1)S(1)} async-done(((bf16[640,4,512]{2,0,1:T(8,128)(2,1)}), bf16[640,4,512]{2,0,1:T(8,128)(2,1)S(1)}, u32[]{:S(2)}, u32[]{:S(2)}) %all-to-all-start.3) | async-done | bytes 2621472 | tf_op jit(solution)/shard_map/all_to_all | solution.py:46
  203.3 0.0 all-gather.6.cloned.1.call-done
  203.3 18.9 %fusion = (bf16[512,2048]{0,1:T(8,128)(2,1)}, f32[512,2048]{0,1:T(8,128)}, f32[512,2048]{0,1:T(8,128)}, f32[512,2048]{0,1:T(8,128)}) fusion(f32[512,2048]{0,1:T(8,128)} %copy.60, f32[512,2048]{0,1:T(8,128)} %copy.56, f32[512,2048]{0,1:T(8,128)} %copy.58, bf16[2560,2048]{1,0:T(8,128)(2,1)} %all-gather.6.cloned.1.call-done, bf16[2560,512]{1,0:T(8,128)(2,1)S(1)} %bitcast.32), kind=kOutput, calls=%fused_computation.13 | convolution fusion | flops 5386534912 | bytes 40370176 | tf_op jit(solution)/shard_map/dot_general | solution.py:48
  222.2 0.0 all-gather.8.cloned.1.call-update
  222.2 3.1 reduce-scatter.5.cloned.1.call-done
  225.3 1.9 convert_element_type.10
  227.2 70.7 %all_to_all.49 = bf16[4,160,1024]{2,1,0:T(8,128)(2,1)S(1)} all-to-all(bf16[4,160,1024]{2,1,0:T(8,128)(2,1)S(1)} %bitcast.30), channel_id=1, replica_groups=mesh['row'=4,'col'=2,'depth'=4] {'row'}, dimensions={0} | all-to-all | bytes 2621440 | tf_op jit(solution)/shard_map/all_to_all | solution.py:39
  297.9 1.3 copy.54
  299.2 13.3 %all_to_all.50 = bf16[2,2,160,1024]{3,1,2,0:T(2,128)(2,1)S(1)} all-to-all(bf16[2,2,160,1024]{3,1,2,0:T(2,128)(2,1)S(1)} %copy.54), channel_id=1, replica_groups=mesh['row'=4,'col'=2,'depth'=4] {'col'}, dimensions={0} | all-to-all | bytes 2621440 | tf_op jit(solution)/shard_map/all_to_all | solution.py:42
  312.5 2.0 copy.55
  314.6 1.8 reshape.30
  316.4 24.3 %reduce-scatter.3.cloned.1.call-done = f32[160,2048]{1,0:T(8,128)} async-done(((f32[640,2048]{1,0:T(8,128)}), f32[160,2048]{1,0:T(8,128)}) %reduce-scatter.3.cloned.1.call-update) | async-done | bytes 1310736 | tf_op jit(solution)/shard_map/reduce_scatter | solution.py:36
  340.7 2.2 convert_element_type.9
  342.9 5.3 %copy.61 = f32[512,2048]{1,0:T(8,128)} copy(f32[512,2048]{0,1:T(8,128)} %get-tuple-element.37) | data formatting | bytes 8388608
  348.3 5.3 %copy.62 = f32[512,2048]{1,0:T(8,128)} copy(f32[512,2048]{0,1:T(8,128)} %get-tuple-element.38) | data formatting | bytes 8388608
  353.6 5.7 %copy.63 = f32[512,2048]{1,0:T(8,128)} copy(f32[512,2048]{0,1:T(8,128)} %get-tuple-element.39) | data formatting | bytes 8388608
  359.4 46.2 %all-gather.8.cloned.1.call-done = bf16[2048,2048]{0,1:T(8,128)(2,1)} async-done(((bf16[512,2048]{0,1:T(8,128)(2,1)}), bf16[2048,2048]{0,1:T(8,128)(2,1)}) %all-gather.8.cloned.1.call-update) | async-done | bytes 8388624 | tf_op jit(solution)/shard_map/all_gather | solution.py:57
  405.6 12.2 %copy.64 = bf16[2048,2048]{1,0:T(8,128)(2,1)} copy(bf16[2048,2048]{0,1:T(8,128)(2,1)} %all-gather.8.cloned.1.call-done) | data formatting | bytes 16777216
  (8 shorter events, 0.4 us)
Async XLA Ops:
  7.2 54.8 %copy-start = (bf16[160,2048]{1,0:T(8,128)(2,1)S(1)}, bf16[160,2048]{1,0:T(8,128)(2,1)}, u32[]{:S(2)}) copy-start(bf16[160,2048]{1,0:T(8,128)(2,1)} %param.8) | copy-start | bytes 1966084
  7.2 78.2 %all-gather.4.cloned.1.call-start = ((), (), s32[]{:S(2)}) async-start(), calls=%async_computation.6 | async-start | bytes 3932160 | tf_op jit(solution)/shard_map/all_gather | solution.py:21
  7.2 20.1 %collective-permute-start = (bf16[160,2048]{1,0:T(8,128)(2,1)}, bf16[160,2048]{1,0:T(8,128)(2,1)S(1)}, u32[]{:S(2)}, u32[]{:S(2)}) collective-permute-start(bf16[160,2048]{1,0:T(8,128)(2,1)} %param.8), channel_id=1, source_target_pairs={{0,8},{8,16},{16,24},{24,0},{1,9},{9,17},{17,25},{25,1},{2,10},{10... | collective-permute-start | bytes 1966088 | tf_op jit(solution)/shard_map/ppermute | solution.py:24
  27.3 17.7 %collective-permute-start.1 = (bf16[160,2048]{1,0:T(8,128)(2,1)S(1)}, bf16[160,2048]{1,0:T(8,128)(2,1)S(1)}, u32[]{:S(2)}, u32[]{:S(2)}) collective-permute-start(bf16[160,2048]{1,0:T(8,128)(2,1)S(1)} %collective-permute-done), channel_id=1, source_target_pairs={{0,8},{8,16},{16,24},{24,0},{1,9},{9,17},{17,25},{25,1},{2,10},{10... | collective-permute-start | bytes 1966088 | tf_op jit(solution)/shard_map/ppermute | solution.py:24
  45.0 16.8 %collective-permute-start.2 = (bf16[160,2048]{1,0:T(8,128)(2,1)S(1)}, bf16[160,2048]{1,0:T(8,128)(2,1)S(1)}, u32[]{:S(2)}, u32[]{:S(2)}) collective-permute-start(bf16[160,2048]{1,0:T(8,128)(2,1)S(1)} %collective-permute-done.1), channel_id=1, source_target_pairs={{0,8},{8,16},{16,24},{24,0},{1,9},{9,17},{17,25},{25,1},{2,10},{10... | collective-permute-start | bytes 1966088 | tf_op jit(solution)/shard_map/ppermute | solution.py:24
  45.0 158.2 %all-gather.6.cloned.1.call-start = ((), (), s32[]{:S(2)}) async-start(), calls=%async_computation.9 | async-start | bytes 13107200 | tf_op jit(solution)/shard_map/all_gather | solution.py:47
  64.5 160.8 %reduce-scatter.5.cloned.1.call-start = ((), (), s32[]{:S(2)}) async-start(), calls=%async_computation.8 | async-start | bytes 7864320 | tf_op jit(solution)/shard_map/reduce_scatter | solution.py:32
  75.7 265.1 %reduce-scatter.3.cloned.1.call-start = ((), (), s32[]{:S(2)}) async-start(), calls=%async_computation.7 | async-start | bytes 6553600 | tf_op jit(solution)/shard_map/reduce_scatter | solution.py:36
  168.3 34.9 %all-to-all-start.3 = ((bf16[640,4,512]{2,0,1:T(8,128)(2,1)}), bf16[640,4,512]{2,0,1:T(8,128)(2,1)S(1)}, u32[]{:S(2)}, u32[]{:S(2)}) async-start(bf16[640,4,512]{2,0,1:T(8,128)(2,1)} %copy.57), calls=%async_computation.5 | async-start | bytes 5242880 | tf_op jit(solution)/shard_map/all_to_all | solution.py:46
  172.0 233.6 %all-gather.8.cloned.1.call-start = ((), (), s32[]{:S(2)}) async-start(), calls=%async_computation.10 | async-start | bytes 10485760 | tf_op jit(solution)/shard_map/all_gather | solution.py:57
Sparse Core Ops, SparseCore 0:
  45.1 40.2 all-gather.3
  87.0 70.1 all-gather.5
  159.5 65.7 reduce-scatter.4
  228.0 112.6 reduce-scatter.2
  342.1 63.4 all-gather.7
